TPU v7x, 128 devices: a whole 4x4x4 slice. The times are simulated.
128 devices in a mesh: dp: 16 (over x, z_hi, core), ctx: 8 (over z_lo, y).
Axes of the slice: x: 4, y: 4, z: 4 (z_hi: 2, z_lo: 2; z = z_hi * 2 + z_lo), core: 2. Of those that a mesh axis runs over, the one named last changes fastest.
Arguments:
- light_flux: float32 [16, 6, 4096], P('dp', None, 'ctx'), may hold values from -6 to 6
- lengths: int32 [16], P('dp'), may hold values from 1024 to 4096, as said below
- offsets: int32 [16, 4096], P('dp', 'ctx'), may hold values from 0 to 3
- start_weight: float32 [512, 3], replicated, may hold values from -3.5 to 3.5
- conv_weight: bfloat16 [2, 1024, 1536], P(None, 'dp'), may hold values from -0.15625 to 0.15625
- gate_bias: float32 [2, 1024], replicated, may hold values from -4 to 4
- mix_first: bfloat16 [1024, 512], P('dp'), may hold values from -0.25 to 0.25
- mix_last: bfloat16 [512, 512], P('dp'), may hold values from -0.25 to 0.25
- end_weight: float32 [6, 512], replicated, may hold values from -0.25 to 0.25
- cotangent: float32 [16, 3, 4096], P('dp', None, 'ctx'), may hold values from -0.0234375 to 0.0234375
Outputs:
- coupled: float32 [16, 3, 4096], P('dp', None, 'ctx')
- grad_start: float32 [512, 3], replicated
- grad_conv: float32 [2, 1024, 1536], P(None, 'dp')
- grad_bias: float32 [2, 1024], replicated
- grad_mix_first: float32 [1024, 512], P('dp')
- grad_mix_last: float32 [512, 512], P('dp')
- grad_end: float32 [6, 512], replicated
Inputs may be any that keep to these rules, and one draw needn't show every extreme that they name: `lengths`: epochs at or past a curve's length are padding; at least one curve has no padding.
All inputs are finite; a program needn't handle non-finite values.
Results may differ from a plain program's by a relative error of at most 0.0091.
Values may be sent and summed in bfloat16 or wider, within the bound.
No kernel may reach another device: no remote copies, remote signals or barrier semaphores. Data moves between devices by JAX's collectives and lax.ppermute only.
A program may use at most 128 MiB of HBM per device.

v0:
```python
import jax
import jax.numpy as jnp
from jax import lax
from jax.sharding import PartitionSpec as P

BUCKETS = 4
highest = lax.Precision.HIGHEST


def from_behind(array, axis, by):
    size = lax.axis_size(axis)
    pairs = [(i, i + by) for i in range(size) if 0 <= i + by < size]
    return lax.ppermute(array, axis, pairs)


def tap_stack(padded, bucket, dilation, reach_len, col_count):
    centre = lax.slice_in_dim(padded, reach_len, reach_len + col_count, axis=1)
    left_tap = lax.slice_in_dim(
        padded, reach_len - dilation, reach_len - dilation + col_count, axis=1
    )
    right_tap = lax.slice_in_dim(
        padded, reach_len + dilation, reach_len + dilation + col_count, axis=1
    )
    for shift_k in range(1, BUCKETS):
        chosen = (bucket == shift_k)[None, :]
        left_start = reach_len - dilation - shift_k
        right_start = reach_len + dilation + shift_k
        left_tap = jnp.where(
            chosen, lax.slice_in_dim(padded, left_start, left_start + col_count, axis=1), left_tap
        )
        right_tap = jnp.where(
            chosen,
            lax.slice_in_dim(padded, right_start, right_start + col_count, axis=1),
            right_tap,
        )
    return jnp.concatenate([left_tap, centre, right_tap], axis=0)


def place_piece(piece, start_col, total_len):
    return jnp.pad(piece, ((0, 0), (start_col, total_len - start_col - piece.shape[1])))


def tap_transpose(d_stacked, bucket, dilation, reach_len, col_count, channels):
    total_len = col_count + 2 * reach_len
    d_left = d_stacked[:channels]
    d_centre = d_stacked[channels : 2 * channels]
    d_right = d_stacked[2 * channels :]
    window = place_piece(d_centre, reach_len, total_len)
    for shift_k in range(BUCKETS):
        chosen = (bucket == shift_k)[None, :]
        left_part = jnp.where(chosen, d_left, 0.0)
        right_part = jnp.where(chosen, d_right, 0.0)
        window = window + place_piece(left_part, reach_len - dilation - shift_k, total_len)
        window = window + place_piece(right_part, reach_len + dilation + shift_k, total_len)
    return window


def gate_forward(preact):
    channels = preact.shape[0] // 2
    return jnp.tanh(preact[:channels]) * jax.nn.sigmoid(preact[channels:])


def gate_backward(preact, d_gated):
    channels = preact.shape[0] // 2
    tangent = jnp.tanh(preact[:channels])
    sigmoid_part = jax.nn.sigmoid(preact[channels:])
    d_upper = d_gated * sigmoid_part * (1.0 - tangent * tangent)
    d_lower = d_gated * tangent * sigmoid_part * (1.0 - sigmoid_part)
    return jnp.concatenate([d_upper, d_lower], axis=0).astype(jnp.bfloat16)


def contract_rows(left_op, right_op, precision=None):
    return lax.dot_general(
        left_op,
        right_op,
        (((1,), (1,)), ((), ())),
        precision=precision,
        preferred_element_type=jnp.float32,
    )


def contract_cols(left_op, right_op, precision=None):
    return lax.dot_general(
        left_op,
        right_op,
        (((0,), (0,)), ((), ())),
        precision=precision,
        preferred_element_type=jnp.float32,
    )


def extend(hidden, reach_len, shard_len):
    pieces_low = []
    pieces_high = []
    remain = reach_len
    distance = 1
    while remain > 0:
        amount = min(shard_len, remain)
        from_low = from_behind(hidden[:, shard_len - amount :], "ctx", distance)
        from_high = from_behind(hidden[:, :amount], "ctx", -distance)
        pieces_low.insert(0, from_low)
        pieces_high.append(from_high)
        remain = remain - amount
        distance = distance + 1
    return jnp.concatenate(pieces_low + [hidden] + pieces_high, axis=1)


def return_rims(grad_window, reach_len, shard_len):
    middle = grad_window[:, reach_len : reach_len + shard_len]
    remain = reach_len
    distance = 1
    end_col = reach_len
    while remain > 0:
        amount = min(shard_len, remain)
        piece_low = grad_window[:, end_col - amount : end_col]
        high_start = reach_len + shard_len + (reach_len - remain)
        piece_high = grad_window[:, high_start : high_start + amount]
        back_low = from_behind(piece_low, "ctx", -distance)
        back_high = from_behind(piece_high, "ctx", distance)
        middle = middle + place_piece(back_low, shard_len - amount, shard_len)
        middle = middle + place_piece(back_high, 0, shard_len)
        end_col = end_col - amount
        remain = remain - amount
        distance = distance + 1
    return middle


def layer_forward(conv_shard, mix_shard, bias_row, stacked):
    full_conv, full_mix = (
        lax.all_gather(conv_shard, "dp", axis=0, tiled=True),
        lax.all_gather(mix_shard, "dp", axis=0, tiled=True),
    )
    preact = jnp.dot(full_conv, stacked, preferred_element_type=jnp.float32) + bias_row[:, None]
    gated = gate_forward(preact).astype(jnp.bfloat16)
    mixed_rows = jnp.dot(full_mix, gated, preferred_element_type=jnp.float32)
    return (preact, gated, mixed_rows, (full_conv, full_mix))


def mix_back(mix_weight, d_mixed):
    return contract_cols(mix_weight, d_mixed)


def conv_back(conv_weight_rows, dz_rows):
    return contract_cols(conv_weight_rows, dz_rows)


def reduce_grad(left_op, right_op):
    full_grad = contract_rows(left_op, right_op)
    summed = lax.psum(full_grad, "ctx")
    return lax.psum_scatter(summed, "dp", scatter_dimension=0, tiled=True)


def local(
    light_flux,
    lengths,
    offsets,
    start_weight,
    conv_weight,
    gate_bias,
    mix_first,
    mix_last,
    end_weight,
    cotangent,
):
    shard_len = light_flux.shape[2]
    half_bands = light_flux.shape[1] // 2
    channels = start_weight.shape[0]
    position = lax.axis_index("ctx") * shard_len + jnp.arange(shard_len, dtype=jnp.int32)
    valid_mask = (position < lengths[0]).astype(jnp.float32)
    bucket = offsets[0]
    first_half = light_flux[0, :half_bands]
    second_half = light_flux[0, half_bands:]
    dilations = (shard_len // 4, shard_len + shard_len // 2)
    reaches = (dilations[0] + BUCKETS - 1, dilations[1] + BUCKETS - 1)
    hidden_first = (jnp.dot(start_weight, first_half, precision=highest) * valid_mask).astype(
        jnp.bfloat16
    )
    stacked_first = tap_stack(
        extend(hidden_first, reaches[0], shard_len), bucket, dilations[0], reaches[0], shard_len
    )
    pre_first, gated_first, mixed_first, kept_first = layer_forward(
        conv_weight[0], mix_first, gate_bias[0], stacked_first
    )
    hidden_second = (
        (hidden_first.astype(jnp.float32) + mixed_first[:channels]) * valid_mask
    ).astype(jnp.bfloat16)
    stacked_second = tap_stack(
        extend(hidden_second, reaches[1], shard_len), bucket, dilations[1], reaches[1], shard_len
    )
    pre_second, gated_second, mixed_second, kept_second = layer_forward(
        conv_weight[1], mix_last, gate_bias[1], stacked_second
    )
    skip_total = mixed_first[channels:] + mixed_second
    end_out = jnp.dot(end_weight, skip_total, precision=highest)
    growth = jnp.exp(end_out[:half_bands])
    coupled = ((growth * second_half + end_out[half_bands:]) * valid_mask)[None]
    d_coupled = cotangent[0] * valid_mask
    d_end = jnp.concatenate([d_coupled * growth * second_half, d_coupled], axis=0)
    grad_end_local = contract_rows(d_end, skip_total, highest)
    d_skip = contract_cols(end_weight, d_end, highest)
    d_skip_b = d_skip.astype(jnp.bfloat16)
    d_gated_second = mix_back(kept_second[1], d_skip_b)
    grad_mix_last = reduce_grad(d_skip_b, gated_second)
    dz_second = gate_backward(pre_second, d_gated_second)
    grad_conv_second = reduce_grad(dz_second, stacked_second)
    bias_second = jnp.sum(dz_second.astype(jnp.float32), axis=1)
    d_stacked_second = conv_back(kept_second[0], dz_second)
    d_window_second = tap_transpose(
        d_stacked_second, bucket, dilations[1], reaches[1], shard_len, channels
    )
    d_field_second = return_rims(d_window_second, reaches[1], shard_len)
    d_mixed_first = jnp.concatenate([d_field_second * valid_mask, d_skip], axis=0).astype(
        jnp.bfloat16
    )
    d_gated_first = mix_back(kept_first[1], d_mixed_first)
    grad_mix_first = reduce_grad(d_mixed_first, gated_first)
    dz_first = gate_backward(pre_first, d_gated_first)
    grad_conv_first = reduce_grad(dz_first, stacked_first)
    bias_first = jnp.sum(dz_first.astype(jnp.float32), axis=1)
    d_stacked_first = conv_back(kept_first[0], dz_first)
    d_window_first = tap_transpose(
        d_stacked_first, bucket, dilations[0], reaches[0], shard_len, channels
    )
    d_hidden_first = d_field_second * valid_mask + return_rims(
        d_window_first, reaches[0], shard_len
    )
    grad_start_local = contract_rows(d_hidden_first * valid_mask, first_half, highest)
    grad_start, grad_bias, grad_end = lax.psum(
        (grad_start_local, jnp.stack([bias_first, bias_second]), grad_end_local), ("dp", "ctx")
    )
    grad_conv = jnp.stack([grad_conv_first, grad_conv_second])
    return (coupled, grad_start, grad_conv, grad_bias, grad_mix_first, grad_mix_last, grad_end)


def solution(mesh):
    in_specs = (
        P("dp", None, "ctx"),
        P("dp"),
        P("dp", "ctx"),
        P(),
        P(None, "dp", None),
        P(),
        P("dp", None),
        P("dp", None),
        P(),
        P("dp", None, "ctx"),
    )
    out_specs = (
        P("dp", None, "ctx"),
        P(),
        P(None, "dp", None),
        P(),
        P("dp", None),
        P("dp", None),
        P(),
    )
    return jax.shard_map(local, mesh=mesh, in_specs=in_specs, out_specs=out_specs, check_vma=False)
```

profile of v0, /device:TPU:1, one launch (start us, length us, event | category | flops | bytes accessed | tf_op | source)
XLA Modules:
  0.0 635.6 jit_solution(13438480193903545730)
XLA Ops:
  13.8 4.0 collective-permute-start
  20.1 3.8 collective-permute-done.1
  23.9 4.0 fusion.43
  28.0 39.5 %all-gather.8.cloned.1.call-done = bf16[1,1024,1536]{2,1,0:T(8,128)(2,1)} async-done(((bf16[1,64,1536]{2,1,0:T(8,128)(2,1)}), bf16[1,1024,1536]{2,1,0:T(8,128)(2,1)}) %all-gather.8.cloned.1.call-update) | async-done | bytes 3145744 | tf_op jit(solution)/shard_map/all_gather | solution.py:130
  67.5 3.7 add_bitcast_fusion.1
  73.0 40.6 %all-gather.6.cloned.1.call-done = bf16[1024,512]{1,0:T(8,128)(2,1)} async-done(((bf16[64,512]{1,0:T(8,128)(2,1)}), bf16[1024,512]{1,0:T(8,128)(2,1)}) %all-gather.6.cloned.1.call-update) | async-done | bytes 1048592 | tf_op jit(solution)/shard_map/all_gather | solution.py:131
  117.1 4.0 collective-permute-start.3
  121.2 4.6 collective-permute-start.2
  127.1 36.2 %all_gather.15 = bf16[512,512]{1,0:T(8,128)(2,1)} all-gather(bf16[32,512]{1,0:T(8,128)(2,1)S(1)} %copy-done.31), channel_id=1, replica_groups=mesh['dp'=16,'ctx'=8] {'dp'}, dimensions={0}, use_global_device_ids=true | all-gather | bytes 557056 | tf_op jit(solution)/shard_map/all_gather | solution.py:131
  166.2 13.4 %all-gather.10.cloned.1.call-done = bf16[1,1024,1536]{2,1,0:T(8,128)(2,1)} async-done(((bf16[1,64,1536]{2,1,0:T(8,128)(2,1)}), bf16[1,1024,1536]{2,1,0:T(8,128)(2,1)}) %all-gather.10.cloned.1.call-update) | async-done | bytes 3145744 | tf_op jit(solution)/shard_map/all_gather | solution.py:130
  179.6 3.9 add_bitcast_fusion
  198.2 5.0 collective-permute-start.7
  207.4 5.7 collective-permute-start.9
  213.1 26.5 %collective-permute-done.8 = f32[512,259]{0,1:T(8,128)S(1)} collective-permute-done((f32[512,259]{0,1:T(8,128)S(1)}, f32[512,259]{0,1:T(8,128)S(1)}, u32[]{:S(2)}, u32[]{:S(2)}) %collective-permute-start.8) | collective-permute-done | bytes 530464 | tf_op jit(solution)/shard_map/ppermute | solution.py:13
  239.5 2.9 fusion.76
  245.4 5.7 fusion.32
  256.2 4.5 fusion.33
  261.9 3.7 convolution_bitcast_fusion
  267.7 10.9 %reduce-scatter.11.cloned.1.call-done = f32[32,512]{1,0:T(8,128)} async-done(((f32[512,512]{1,0:T(8,128)}), f32[32,512]{1,0:T(8,128)}) %reduce-scatter.11.cloned.1.call-update) | async-done | bytes 65552 | tf_op jit(solution)/shard_map/reduce_scatter | solution.py:150
  278.6 74.3 %reduce-scatter.9.cloned.1.call-done = f32[64,512]{1,0:T(8,128)} async-done(((f32[1024,512]{1,0:T(8,128)}), f32[64,512]{1,0:T(8,128)}) %reduce-scatter.9.cloned.1.call-update) | async-done | bytes 131088 | tf_op jit(solution)/shard_map/reduce_scatter | solution.py:150
  352.9 93.9 %reduce-scatter.7.cloned.1.call-done = f32[64,1536]{1,0:T(8,128)} async-done(((f32[1024,1536]{1,0:T(8,128)}), f32[64,1536]{1,0:T(8,128)}) %reduce-scatter.7.cloned.1.call-update) | async-done | bytes 393232 | tf_op jit(solution)/shard_map/reduce_scatter | solution.py:150
  446.8 93.0 %reduce-scatter.5.cloned.1.call-done = f32[64,1536]{1,0:T(8,128)} async-done(((f32[1024,1536]{1,0:T(8,128)}), f32[64,1536]{1,0:T(8,128)}) %reduce-scatter.5.cloned.1.call-update) | async-done | bytes 393232 | tf_op jit(solution)/shard_map/reduce_scatter | solution.py:150
  541.3 4.0 collective-permute-start.11
  549.9 73.7 %all-reduce.22 = (f32[512,3]{0,1:T(4,128)}, f32[2,1024]{1,0:T(2,128)}, f32[6,512]{1,0:T(8,128)}) all-reduce(f32[512,3]{0,1:T(4,128)S(1)} %fusion.15, f32[2,1024]{1,0:T(2,128)S(1)} %pad_maximum_fusion.22, f32[6,512]{1,0:T(8,128)S(1)} %fusion.55), channel_id=1, replica_groups=mesh['dp'=16,'ctx'=8] {'dp','ctx'}, use_global_device_ids=true, to_apply=%region_0.1 | all-reduce | flops 6656 | bytes 53248 | tf_op jit(solution)/shard_map/psum | solution.py:228
  (145 shorter events, 58.7 us)
Async XLA Ops:
  7.2 177.9 %copy-start = (f32[6,512]{1,0:T(8,128)S(1)}, f32[6,512]{1,0:T(8,128)}, u32[]{:S(2)}) copy-start(f32[6,512]{1,0:T(8,128)} %param.18) | copy-start | bytes 36868
  7.2 60.3 %all-gather.8.cloned.1.call-start = ((), (), s32[]{:S(2)}) async-start(), calls=%async_computation.5 | async-start | bytes 3342336 | tf_op jit(solution)/shard_map/all_gather | solution.py:130
  9.1 104.5 %all-gather.6.cloned.1.call-start = ((), (), s32[]{:S(2)}) async-start(), calls=%async_computation.4 | async-start | bytes 1114112 | tf_op jit(solution)/shard_map/all_gather | solution.py:131
  9.8 169.8 %all-gather.10.cloned.1.call-start = ((), (), s32[]{:S(2)}) async-start(), calls=%async_computation.6 | async-start | bytes 3342336 | tf_op jit(solution)/shard_map/all_gather | solution.py:130
  10.6 268.1 %reduce-scatter.11.cloned.1.call-start = ((), (), s32[]{:S(2)}) async-start(), calls=%async_computation.10 | async-start | bytes 1114112 | tf_op jit(solution)/shard_map/reduce_scatter | solution.py:150
  13.7 101.8 %copy-start.3 = (bf16[512,512]{0,1:T(8,128)(2,1)}, bf16[512,512]{0,1:T(8,128)(2,1)S(1)}, u32[]{:S(2)}) copy-start(bf16[512,512]{0,1:T(8,128)(2,1)S(1)} %fusion.11) | copy-start | bytes 1572868
  13.8 6.4 collective-permute-start
  17.8 6.1 collective-permute-start.1
  115.8 47.5 %collective-permute-start.4 = (bf16[512,512]{0,1:T(8,128)(2,1)S(1)}, bf16[512,512]{0,1:T(8,128)(2,1)S(1)}, u32[]{:S(2)}, u32[]{:S(2)}) collective-permute-start(bf16[512,512]{0,1:T(8,128)(2,1)S(1)} %fusion.25), channel_id=1, source_target_pairs={{1,0},{2,1},{3,2},{4,3},{5,4},{6,5},{7,6},{9,8},{10,9},{11,10},{12... | collective-permute-start | bytes 1572872 | tf_op jit(solution)/shard_map/ppermute | solution.py:13
  117.1 46.3 %collective-permute-start.3 = (bf16[512,512]{0,1:T(8,128)(2,1)S(1)}, bf16[512,512]{0,1:T(8,128)(2,1)S(1)}, u32[]{:S(2)}, u32[]{:S(2)}) collective-permute-start(bf16[512,512]{0,1:T(8,128)(2,1)S(1)} %fusion.25), channel_id=1, source_target_pairs={{0,1},{1,2},{2,3},{3,4},{4,5},{5,6},{6,7},{8,9},{9,10},{10,11},{11... | collective-permute-start | bytes 1572872 | tf_op jit(solution)/shard_map/ppermute | solution.py:13
  121.2 42.2 %collective-permute-start.2 = (bf16[512,259]{0,1:T(8,128)(2,1)S(1)}, bf16[512,259]{0,1:T(8,128)(2,1)S(1)}, u32[]{:S(2)}, u32[]{:S(2)}) collective-permute-start(bf16[512,259]{0,1:T(8,128)(2,1)S(1)} %get-tuple-element.71), channel_id=1, source_target_pairs={{0,2},{1,3},{2,4},{3,5},{4,6},{5,7},{8,10},{9,11},{10,12},{11,13},... | collective-permute-start | bytes 795656 | tf_op jit(solution)/shard_map/ppermute | solution.py:13
  125.8 37.6 %collective-permute-start.5 = (bf16[512,259]{0,1:T(8,128)(2,1)S(1)}, bf16[512,259]{0,1:T(8,128)(2,1)S(1)}, u32[]{:S(2)}, u32[]{:S(2)}) collective-permute-start(bf16[512,259]{0,1:T(8,128)(2,1)S(1)} %get-tuple-element.72), channel_id=1, source_target_pairs={{2,0},{3,1},{4,2},{5,3},{6,4},{7,5},{10,8},{11,9},{12,10},{13,11},... | collective-permute-start | bytes 795656 | tf_op jit(solution)/shard_map/ppermute | solution.py:13
  197.0 42.6 %collective-permute-start.6 = (f32[512,512]{0,1:T(8,128)}, f32[512,512]{0,1:T(8,128)S(1)}, u32[]{:S(2)}, u32[]{:S(2)}) collective-permute-start(f32[512,512]{0,1:T(8,128)} %get-tuple-element.27), channel_id=1, source_target_pairs={{1,0},{2,1},{3,2},{4,3},{5,4},{6,5},{7,6},{9,8},{10,9},{11,10},{12... | collective-permute-start | bytes 3145736 | tf_op jit(solution)/shard_map/ppermute | solution.py:13
  198.2 41.3 %collective-permute-start.7 = (f32[512,512]{0,1:T(8,128)}, f32[512,512]{0,1:T(8,128)}, u32[]{:S(2)}, u32[]{:S(2)}) collective-permute-start(f32[512,512]{0,1:T(8,128)} %get-tuple-element.28), channel_id=1, source_target_pairs={{0,1},{1,2},{2,3},{3,4},{4,5},{5,6},{6,7},{8,9},{9,10},{10,11},{11... | collective-permute-start | bytes 3145736 | tf_op jit(solution)/shard_map/ppermute | solution.py:13
  204.7 148.2 %reduce-scatter.9.cloned.1.call-start = ((), (), s32[]{:S(2)}) async-start(), calls=%async_computation.9 | async-start | bytes 2228224 | tf_op jit(solution)/shard_map/reduce_scatter | solution.py:150
  206.1 33.4 %collective-permute-start.8 = (f32[512,259]{0,1:T(8,128)S(1)}, f32[512,259]{0,1:T(8,128)S(1)}, u32[]{:S(2)}, u32[]{:S(2)}) collective-permute-start(f32[512,259]{0,1:T(8,128)S(1)} %get-tuple-element.29), channel_id=1, source_target_pairs={{2,0},{3,1},{4,2},{5,3},{6,4},{7,5},{10,8},{11,9},{12,10},{13,11},... | collective-permute-start | bytes 1591304 | tf_op jit(solution)/shard_map/ppermute | solution.py:13
  207.4 32.1 %collective-permute-start.9 = (f32[512,259]{0,1:T(8,128)S(1)}, f32[512,259]{0,1:T(8,128)S(1)}, u32[]{:S(2)}, u32[]{:S(2)}) collective-permute-start(f32[512,259]{0,1:T(8,128)S(1)} %get-tuple-element.30), channel_id=1, source_target_pairs={{0,2},{1,3},{2,4},{3,5},{4,6},{5,7},{8,10},{9,11},{10,12},{11,13},... | collective-permute-start | bytes 1591304 | tf_op jit(solution)/shard_map/ppermute | solution.py:13
  245.3 201.5 %reduce-scatter.7.cloned.1.call-start = ((), (), s32[]{:S(2)}) async-start(), calls=%async_computation.8 | async-start | bytes 6684672 | tf_op jit(solution)/shard_map/reduce_scatter | solution.py:150
  251.2 288.6 %reduce-scatter.5.cloned.1.call-start = ((), (), s32[]{:S(2)}) async-start(), calls=%async_computation.7 | async-start | bytes 6684672 | tf_op jit(solution)/shard_map/reduce_scatter | solution.py:150
  260.8 362.9 %all-reduce.26.cloned.1.call-start = ((), (), s32[]{:S(2)}) async-start(), calls=%async_computation.11 | async-start | bytes 1966080 | tf_op jit(solution)/shard_map/psum | solution.py:149
  267.7 278.9 %copy-start.17 = (bf16[512,512]{0,1:T(8,128)(2,1)S(1)}, bf16[512,512]{0,1:T(8,128)(2,1)}, u32[]{:S(2)}) copy-start(bf16[512,512]{0,1:T(8,128)(2,1)} %copy-done.16) | copy-start | bytes 1572868
  539.9 8.3 %collective-permute-start.10 = (f32[512,131]{0,1:T(8,128)S(1)}, f32[512,131]{0,1:T(8,128)S(1)}, u32[]{:S(2)}, u32[]{:S(2)}) collective-permute-start(f32[512,131]{0,1:T(8,128)S(1)} %get-tuple-element.67), channel_id=1, source_target_pairs={{1,0},{2,1},{3,2},{4,3},{5,4},{6,5},{7,6},{9,8},{10,9},{11,10},{12... | collective-permute-start | bytes 804872 | tf_op jit(solution)/shard_map/ppermute | solution.py:13
  541.3 7.7 %collective-permute-start.11 = (f32[512,131]{0,1:T(8,128)S(1)}, f32[512,131]{0,1:T(8,128)S(1)}, u32[]{:S(2)}, u32[]{:S(2)}) collective-permute-start(f32[512,131]{0,1:T(8,128)S(1)} %get-tuple-element.68), channel_id=1, source_target_pairs={{0,1},{1,2},{2,3},{3,4},{4,5},{5,6},{6,7},{8,9},{9,10},{10,11},{11... | collective-permute-start | bytes 804872 | tf_op jit(solution)/shard_map/ppermute | solution.py:13
  549.1 79.7 %copy-start.1 = (f32[6,512]{1,0:T(8,128)S(1)}, f32[6,512]{1,0:T(8,128)}, u32[]{:S(2)}) copy-start(f32[6,512]{1,0:T(8,128)} %param.18) | copy-start | bytes 36868
  (32 other events, 345.2 us)
Sparse Core Ops, SparseCore 0:
  11.0 56.4 all-gather.7
  69.9 43.6 all-gather.5
  116.0 63.5 all-gather.9
  204.8 73.7 reduce-scatter.10
  282.9 69.9 reduce-scatter.8
  357.5 89.2 reduce-scatter.6
  451.5 88.2 reduce-scatter.4
  542.8 71.9 all-reduce.25
where the time goes:
time: 637 us; the launch traced here: 636 us
  waiting for transfers between devices  400 us (63%)
  blocking collectives  110 us (17%)
  matrix products  38.1 us (6%)
  starting transfers between devices  35.7 us (6%)
  local copies, waits for them, and re-layouts  18.5 us (3%)
  other arithmetic  17.6 us (3%)
  between operations  15.4 us (2%)
    reduce_scatter x4, waiting for transfers between devices, reduce_grad(): return lax.psum_scatter(summed, 'dp', scatter_dimension=0, tiled=True)  272 us
    psum x1, blocking collectives, local(): lax.psum((grad_start_local, jnp.stack([bias_first, bias_second]), grad_en...  73.7 us
    all_gather x2, waiting for transfers between devices, layer_forward(): lax.all_gather(conv_shard, 'dp', axis=0, tiled=True)  52.9 us
    all_gather x1, waiting for transfers between devices, layer_forward(): lax.all_gather(mix_shard, 'dp', axis=0, tiled=True)  40.6 us
    all_gather x1, blocking collectives, layer_forward(): lax.all_gather(mix_shard, 'dp', axis=0, tiled=True)  36.2 us
    ppermute x12, starting transfers between devices, from_behind(): return lax.ppermute(array, axis, pairs)  35.2 us
    ppermute x12, waiting for transfers between devices, from_behind(): return lax.ppermute(array, axis, pairs)  33.3 us
    dot_general x6, matrix products, contract_rows(): lax.dot_general(left_op, right_op, (((1,), (1,)), ((), ())), precision=pr...  15.2 us
  transfers between devices with their start and end apart: 20, of which 12 were waited for; matrix products, arithmetic and copies ran while one was open for 7% of the time, Pallas kernels for 0%

commit v1 on v0

--- a/solution.py
+++ b/solution.py
@@ -1,3 +1,4 @@
+import functools
 import jax
 import jax.numpy as jnp
 from jax import lax
@@ -5,6 +6,14 @@
 
 BUCKETS = 4
 highest = lax.Precision.HIGHEST
+
+
+def form_fields(my_data, axis_key, bus_axis):
+    low = lax.psum(my_data, axis_key)
+    return lax.psum(low, bus_axis)
+
+
+note_loads_on = functools.partial(form_fields, axis_key="ctx", bus_axis="dp")
 
 
 def from_behind(array, axis, by):
@@ -225,8 +234,8 @@
         d_window_first, reaches[0], shard_len
     )
     grad_start_local = contract_rows(d_hidden_first * valid_mask, first_half, highest)
-    grad_start, grad_bias, grad_end = lax.psum(
-        (grad_start_local, jnp.stack([bias_first, bias_second]), grad_end_local), ("dp", "ctx")
+    grad_start, grad_bias, grad_end = note_loads_on(
+        (grad_start_local, jnp.stack([bias_first, bias_second]), grad_end_local)
     )
     grad_conv = jnp.stack([grad_conv_first, grad_conv_second])
     return (coupled, grad_start, grad_conv, grad_bias, grad_mix_first, grad_mix_last, grad_end)

time: 637 us -> 668 us (1.049)
  blocking collectives: 110 us -> 135 us
    psum x1 -> x2, blocking collectives: 73.7 us -> 98.7 us  [the longest x1 70.1 us: form_fields(): return lax.psum(low, bus_axis)]
where the time goes in v1:
time: 668 us; the launch traced here: 660 us
  waiting for transfers between devices  400 us (60%)
  blocking collectives  135 us (20%)
  matrix products  38.1 us (6%)
  starting transfers between devices  35.7 us (5%)
  local copies, waits for them, and re-layouts  18.5 us (3%)
  other arithmetic  17.6 us (3%)
  between operations  15.4 us (2%)
    reduce_scatter x4, waiting for transfers between devices, reduce_grad(): return lax.psum_scatter(summed, 'dp', scatter_dimension=0, tiled=True)  272 us
    psum x1, blocking collectives, form_fields(): return lax.psum(low, bus_axis)  70.1 us
    all_gather x2, waiting for transfers between devices, layer_forward(): lax.all_gather(conv_shard, 'dp', axis=0, tiled=True)  52.9 us
    all_gather x1, waiting for transfers between devices, layer_forward(): lax.all_gather(mix_shard, 'dp', axis=0, tiled=True)  40.5 us
    all_gather x1, blocking collectives, layer_forward(): lax.all_gather(mix_shard, 'dp', axis=0, tiled=True)  36.2 us
    ppermute x12, starting transfers between devices, from_behind(): return lax.ppermute(array, axis, pairs)  35.2 us
    ppermute x12, waiting for transfers between devices, from_behind(): return lax.ppermute(array, axis, pairs)  33.1 us
    psum x1, blocking collectives, form_fields(): low = lax.psum(my_data, axis_key)  28.6 us
  transfers between devices with their start and end apart: 20, of which 12 were waited for; matrix products, arithmetic and copies ran while one was open for 7% of the time, Pallas kernels for 0%

profile of v1, /device:TPU:1, one launch (start us, length us, event | category | flops | bytes accessed | tf_op | source)
XLA Modules:
  0.0 660.1 jit_solution(1660582100547987181)
XLA Ops:
  13.7 4.0 collective-permute-start
  20.1 3.8 collective-permute-done.1
  23.9 4.0 fusion.43
  28.0 39.5 %all-gather.8.cloned.1.call-done = bf16[1,1024,1536]{2,1,0:T(8,128)(2,1)} async-done(((bf16[1,64,1536]{2,1,0:T(8,128)(2,1)}), bf16[1,1024,1536]{2,1,0:T(8,128)(2,1)}) %all-gather.8.cloned.1.call-update) | async-done | bytes 3145744 | tf_op jit(solution)/shard_map/all_gather | solution.py:139
  67.5 3.7 add_bitcast_fusion.1
  73.0 40.5 %all-gather.6.cloned.1.call-done = bf16[1024,512]{1,0:T(8,128)(2,1)} async-done(((bf16[64,512]{1,0:T(8,128)(2,1)}), bf16[1024,512]{1,0:T(8,128)(2,1)}) %all-gather.6.cloned.1.call-update) | async-done | bytes 1048592 | tf_op jit(solution)/shard_map/all_gather | solution.py:140
  117.1 4.0 collective-permute-start.3
  121.2 4.6 collective-permute-start.2
  127.1 36.2 %all_gather.15 = bf16[512,512]{1,0:T(8,128)(2,1)} all-gather(bf16[32,512]{1,0:T(8,128)(2,1)S(1)} %copy-done.31), channel_id=1, replica_groups=mesh['dp'=16,'ctx'=8] {'dp'}, dimensions={0}, use_global_device_ids=true | all-gather | bytes 557056 | tf_op jit(solution)/shard_map/all_gather | solution.py:140
  166.2 13.4 %all-gather.10.cloned.1.call-done = bf16[1,1024,1536]{2,1,0:T(8,128)(2,1)} async-done(((bf16[1,64,1536]{2,1,0:T(8,128)(2,1)}), bf16[1,1024,1536]{2,1,0:T(8,128)(2,1)}) %all-gather.10.cloned.1.call-update) | async-done | bytes 3145744 | tf_op jit(solution)/shard_map/all_gather | solution.py:139
  179.6 3.9 add_bitcast_fusion
  198.2 5.0 collective-permute-start.7
  207.3 5.7 collective-permute-start.9
  213.0 26.5 %collective-permute-done.8 = f32[512,259]{0,1:T(8,128)S(1)} collective-permute-done((f32[512,259]{0,1:T(8,128)S(1)}, f32[512,259]{0,1:T(8,128)S(1)}, u32[]{:S(2)}, u32[]{:S(2)}) %collective-permute-start.8) | collective-permute-done | bytes 530464 | tf_op jit(solution)/shard_map/ppermute | solution.py:22
  245.4 5.7 fusion.32
  256.2 4.5 fusion.33
  261.9 3.7 convolution_bitcast_fusion
  267.7 10.9 %reduce-scatter.11.cloned.1.call-done = f32[32,512]{1,0:T(8,128)} async-done(((f32[512,512]{1,0:T(8,128)}), f32[32,512]{1,0:T(8,128)}) %reduce-scatter.11.cloned.1.call-update) | async-done | bytes 65552 | tf_op jit(solution)/shard_map/reduce_scatter | solution.py:159
  278.6 74.3 %reduce-scatter.9.cloned.1.call-done = f32[64,512]{1,0:T(8,128)} async-done(((f32[1024,512]{1,0:T(8,128)}), f32[64,512]{1,0:T(8,128)}) %reduce-scatter.9.cloned.1.call-update) | async-done | bytes 131088 | tf_op jit(solution)/shard_map/reduce_scatter | solution.py:159
  352.9 93.8 %reduce-scatter.7.cloned.1.call-done = f32[64,1536]{1,0:T(8,128)} async-done(((f32[1024,1536]{1,0:T(8,128)}), f32[64,1536]{1,0:T(8,128)}) %reduce-scatter.7.cloned.1.call-update) | async-done | bytes 393232 | tf_op jit(solution)/shard_map/reduce_scatter | solution.py:159
  446.7 92.9 %reduce-scatter.5.cloned.1.call-done = f32[64,1536]{1,0:T(8,128)} async-done(((f32[1024,1536]{1,0:T(8,128)}), f32[64,1536]{1,0:T(8,128)}) %reduce-scatter.5.cloned.1.call-update) | async-done | bytes 393232 | tf_op jit(solution)/shard_map/reduce_scatter | solution.py:159
  541.2 4.0 collective-permute-start.11
  549.5 28.6 %all-reduce.23 = (f32[512,3]{0,1:T(4,128)S(1)}, f32[2,1024]{1,0:T(2,128)S(1)}, f32[6,512]{1,0:T(8,128)S(1)}) all-reduce(f32[512,3]{0,1:T(4,128)S(1)} %fusion.15, f32[2,1024]{1,0:T(2,128)S(1)} %pad_maximum_fusion.22, f32[6,512]{1,0:T(8,128)S(1)} %fusion.55), channel_id=1, replica_groups=mesh['dp'=16,'ctx'=8] {'ctx'}, use_global_device_ids=true, to_apply=%region_0.1 | all-reduce | flops 6656 | bytes 53248 | tf_op jit(solution)/shard_map/psum | solution.py:12
  578.1 70.1 %all-reduce.22 = (f32[512,3]{0,1:T(4,128)}, f32[2,1024]{1,0:T(2,128)}, f32[6,512]{1,0:T(8,128)}) all-reduce(f32[512,3]{0,1:T(4,128)S(1)} %get-tuple-element.21, f32[2,1024]{1,0:T(2,128)S(1)} %get-tuple-element.22, f32[6,512]{1,0:T(8,128)S(1)} %get-tuple-element.23), channel_id=1, replica_groups=mesh['dp'=16,'ctx'=8] {'dp'}, use_global_device_ids=true, to_apply=%region_1.2 | all-reduce | flops 6656 | bytes 53248 | tf_op jit(solution)/shard_map/psum | solution.py:13
  (146 shorter events, 61.3 us)
Async XLA Ops:
  7.2 177.9 %copy-start = (f32[6,512]{1,0:T(8,128)S(1)}, f32[6,512]{1,0:T(8,128)}, u32[]{:S(2)}) copy-start(f32[6,512]{1,0:T(8,128)} %param.18) | copy-start | bytes 36868
  7.2 60.3 %all-gather.8.cloned.1.call-start = ((), (), s32[]{:S(2)}) async-start(), calls=%async_computation.5 | async-start | bytes 3342336 | tf_op jit(solution)/shard_map/all_gather | solution.py:139
  9.1 104.5 %all-gather.6.cloned.1.call-start = ((), (), s32[]{:S(2)}) async-start(), calls=%async_computation.4 | async-start | bytes 1114112 | tf_op jit(solution)/shard_map/all_gather | solution.py:140
  9.8 169.8 %all-gather.10.cloned.1.call-start = ((), (), s32[]{:S(2)}) async-start(), calls=%async_computation.6 | async-start | bytes 3342336 | tf_op jit(solution)/shard_map/all_gather | solution.py:139
  10.5 268.1 %reduce-scatter.11.cloned.1.call-start = ((), (), s32[]{:S(2)}) async-start(), calls=%async_computation.10 | async-start | bytes 1114112 | tf_op jit(solution)/shard_map/reduce_scatter | solution.py:159
  13.7 101.8 %copy-start.3 = (bf16[512,512]{0,1:T(8,128)(2,1)}, bf16[512,512]{0,1:T(8,128)(2,1)S(1)}, u32[]{:S(2)}) copy-start(bf16[512,512]{0,1:T(8,128)(2,1)S(1)} %fusion.11) | copy-start | bytes 1572868
  13.7 6.4 collective-permute-start
  17.8 6.1 collective-permute-start.1
  115.8 47.5 %collective-permute-start.4 = (bf16[512,512]{0,1:T(8,128)(2,1)S(1)}, bf16[512,512]{0,1:T(8,128)(2,1)S(1)}, u32[]{:S(2)}, u32[]{:S(2)}) collective-permute-start(bf16[512,512]{0,1:T(8,128)(2,1)S(1)} %fusion.25), channel_id=1, source_target_pairs={{1,0},{2,1},{3,2},{4,3},{5,4},{6,5},{7,6},{9,8},{10,9},{11,10},{12... | collective-permute-start | bytes 1572872 | tf_op jit(solution)/shard_map/ppermute | solution.py:22
  117.1 46.3 %collective-permute-start.3 = (bf16[512,512]{0,1:T(8,128)(2,1)S(1)}, bf16[512,512]{0,1:T(8,128)(2,1)S(1)}, u32[]{:S(2)}, u32[]{:S(2)}) collective-permute-start(bf16[512,512]{0,1:T(8,128)(2,1)S(1)} %fusion.25), channel_id=1, source_target_pairs={{0,1},{1,2},{2,3},{3,4},{4,5},{5,6},{6,7},{8,9},{9,10},{10,11},{11... | collective-permute-start | bytes 1572872 | tf_op jit(solution)/shard_map/ppermute | solution.py:22
  121.2 42.2 %collective-permute-start.2 = (bf16[512,259]{0,1:T(8,128)(2,1)S(1)}, bf16[512,259]{0,1:T(8,128)(2,1)S(1)}, u32[]{:S(2)}, u32[]{:S(2)}) collective-permute-start(bf16[512,259]{0,1:T(8,128)(2,1)S(1)} %get-tuple-element.74), channel_id=1, source_target_pairs={{0,2},{1,3},{2,4},{3,5},{4,6},{5,7},{8,10},{9,11},{10,12},{11,13},... | collective-permute-start | bytes 795656 | tf_op jit(solution)/shard_map/ppermute | solution.py:22
  125.8 37.6 %collective-permute-start.5 = (bf16[512,259]{0,1:T(8,128)(2,1)S(1)}, bf16[512,259]{0,1:T(8,128)(2,1)S(1)}, u32[]{:S(2)}, u32[]{:S(2)}) collective-permute-start(bf16[512,259]{0,1:T(8,128)(2,1)S(1)} %get-tuple-element.75), channel_id=1, source_target_pairs={{2,0},{3,1},{4,2},{5,3},{6,4},{7,5},{10,8},{11,9},{12,10},{13,11},... | collective-permute-start | bytes 795656 | tf_op jit(solution)/shard_map/ppermute | solution.py:22
  196.9 42.6 %collective-permute-start.6 = (f32[512,512]{0,1:T(8,128)}, f32[512,512]{0,1:T(8,128)S(1)}, u32[]{:S(2)}, u32[]{:S(2)}) collective-permute-start(f32[512,512]{0,1:T(8,128)} %get-tuple-element.30), channel_id=1, source_target_pairs={{1,0},{2,1},{3,2},{4,3},{5,4},{6,5},{7,6},{9,8},{10,9},{11,10},{12... | collective-permute-start | bytes 3145736 | tf_op jit(solution)/shard_map/ppermute | solution.py:22
  198.2 41.3 %collective-permute-start.7 = (f32[512,512]{0,1:T(8,128)}, f32[512,512]{0,1:T(8,128)}, u32[]{:S(2)}, u32[]{:S(2)}) collective-permute-start(f32[512,512]{0,1:T(8,128)} %get-tuple-element.31), channel_id=1, source_target_pairs={{0,1},{1,2},{2,3},{3,4},{4,5},{5,6},{6,7},{8,9},{9,10},{10,11},{11... | collective-permute-start | bytes 3145736 | tf_op jit(solution)/shard_map/ppermute | solution.py:22
  204.7 148.2 %reduce-scatter.9.cloned.1.call-start = ((), (), s32[]{:S(2)}) async-start(), calls=%async_computation.9 | async-start | bytes 2228224 | tf_op jit(solution)/shard_map/reduce_scatter | solution.py:159
  206.0 33.5 %collective-permute-start.8 = (f32[512,259]{0,1:T(8,128)S(1)}, f32[512,259]{0,1:T(8,128)S(1)}, u32[]{:S(2)}, u32[]{:S(2)}) collective-permute-start(f32[512,259]{0,1:T(8,128)S(1)} %get-tuple-element.32), channel_id=1, source_target_pairs={{2,0},{3,1},{4,2},{5,3},{6,4},{7,5},{10,8},{11,9},{12,10},{13,11},... | collective-permute-start | bytes 1591304 | tf_op jit(solution)/shard_map/ppermute | solution.py:22
  207.3 32.2 %collective-permute-start.9 = (f32[512,259]{0,1:T(8,128)S(1)}, f32[512,259]{0,1:T(8,128)S(1)}, u32[]{:S(2)}, u32[]{:S(2)}) collective-permute-start(f32[512,259]{0,1:T(8,128)S(1)} %get-tuple-element.33), channel_id=1, source_target_pairs={{0,2},{1,3},{2,4},{3,5},{4,6},{5,7},{8,10},{9,11},{10,12},{11,13},... | collective-permute-start | bytes 1591304 | tf_op jit(solution)/shard_map/ppermute | solution.py:22
  245.3 201.4 %reduce-scatter.7.cloned.1.call-start = ((), (), s32[]{:S(2)}) async-start(), calls=%async_computation.8 | async-start | bytes 6684672 | tf_op jit(solution)/shard_map/reduce_scatter | solution.py:159
  251.1 288.5 %reduce-scatter.5.cloned.1.call-start = ((), (), s32[]{:S(2)}) async-start(), calls=%async_computation.7 | async-start | bytes 6684672 | tf_op jit(solution)/shard_map/reduce_scatter | solution.py:159
  260.7 387.5 %all-reduce.27.cloned.1.call-start = ((), (), s32[]{:S(2)}) async-start(), calls=%async_computation.11 | async-start | bytes 1966080 | tf_op jit(solution)/shard_map/psum | solution.py:158
  267.7 278.7 %copy-start.17 = (bf16[512,512]{0,1:T(8,128)(2,1)S(1)}, bf16[512,512]{0,1:T(8,128)(2,1)}, u32[]{:S(2)}) copy-start(bf16[512,512]{0,1:T(8,128)(2,1)} %copy-done.16) | copy-start | bytes 1572868
  539.7 8.2 %collective-permute-start.10 = (f32[512,131]{0,1:T(8,128)S(1)}, f32[512,131]{0,1:T(8,128)S(1)}, u32[]{:S(2)}, u32[]{:S(2)}) collective-permute-start(f32[512,131]{0,1:T(8,128)S(1)} %get-tuple-element.70), channel_id=1, source_target_pairs={{1,0},{2,1},{3,2},{4,3},{5,4},{6,5},{7,6},{9,8},{10,9},{11,10},{12... | collective-permute-start | bytes 804872 | tf_op jit(solution)/shard_map/ppermute | solution.py:22
  541.2 7.5 %collective-permute-start.11 = (f32[512,131]{0,1:T(8,128)S(1)}, f32[512,131]{0,1:T(8,128)S(1)}, u32[]{:S(2)}, u32[]{:S(2)}) collective-permute-start(f32[512,131]{0,1:T(8,128)S(1)} %get-tuple-element.71), channel_id=1, source_target_pairs={{0,1},{1,2},{2,3},{3,4},{4,5},{5,6},{6,7},{8,9},{9,10},{10,11},{11... | collective-permute-start | bytes 804872 | tf_op jit(solution)/shard_map/ppermute | solution.py:22
  548.6 104.6 %copy-start.1 = (f32[6,512]{1,0:T(8,128)S(1)}, f32[6,512]{1,0:T(8,128)}, u32[]{:S(2)}) copy-start(f32[6,512]{1,0:T(8,128)} %param.18) | copy-start | bytes 36868
  (32 other events, 344.9 us)
Sparse Core Ops, SparseCore 0:
  11.0 56.4 all-gather.7
  69.9 43.6 all-gather.5
  116.0 63.5 all-gather.9
  204.8 73.8 reduce-scatter.10
  282.9 69.9 reduce-scatter.8
  357.5 89.2 reduce-scatter.6
  451.4 88.1 reduce-scatter.4
  542.6 72.0 all-reduce.26
